TPU v7x, 256 devices: a whole 4x4x8 slice. The times are simulated.
256 devices in a mesh: ka: 32 (over x_hi, z, core), band: 8 (over x_lo, y).
Axes of the slice: x: 4 (x_hi: 2, x_lo: 2; x = x_hi * 2 + x_lo), y: 4, z: 8, core: 2. Of those that a mesh axis runs over, the one named last changes fastest.
Arguments:
- valence_orbitals: bfloat16 [32, 32, 64, 64, 128], P('ka', None, None, 'band'), may hold values from -6 to 6
- conduction_orbitals: bfloat16 [32, 1, 64, 64, 128], P(None, None, 'ka', 'band'), may hold values from -6 to 6
- valence_energy: float32 [32, 32], P('ka'), may hold values from -1.5 to -0.1
- conduction_energy: float32 [32, 1], replicated, may hold values from 0.1 to 1.5
- valence_select: int32 [32, 16], P('ka'), may hold values from 0 to 31, as said below
- shifted_index: int32 [32], replicated, may hold values from 0 to 31, each once
- wave_vectors: int32 [3, 2048], replicated, may hold values from -16 to 15
- frequency: float32 [1], replicated, may hold values from 0.3 to 1
Outputs:
- chi_zero: float32 [2, 2048, 2048], P(None, ('ka', 'band'))
Inputs may be any that keep to these rules, and one draw needn't show every extreme that they name: `valence_select`: each row holds 16 different band numbers. `shifted_index`: every k point is the partner of exactly one k point.
All inputs are finite; a program needn't handle non-finite values.
Results may differ from a plain program's by a relative error of at most 0.025.
Values may be sent and summed in bfloat16 or wider, within the bound.
No kernel may reach another device: no remote copies, remote signals or barrier semaphores. Data moves between devices by JAX's collectives and lax.ppermute only.
A program may use at most 256 MiB of HBM per device.

v0:
```python
import math
import jax
import jax.numpy as jnp
from jax import lax
from jax.sharding import PartitionSpec as P


def depth_matrix(grid_size):
    positions = jnp.arange(grid_size, dtype=jnp.int32)
    phase_index = positions[:, None] * positions[None, :] % grid_size
    angle_value = phase_index.astype(jnp.float32) * (2.0 * math.pi / grid_size)
    cosine = jnp.cos(angle_value)
    sine_part = jnp.sin(angle_value)
    upper_half = jnp.concatenate([cosine, -sine_part], axis=1)
    lower_half = jnp.concatenate([sine_part, cosine], axis=1)
    return jnp.concatenate([upper_half, lower_half], axis=0).astype(jnp.bfloat16)


def column_matrix(grid_size):
    positions = jnp.arange(grid_size, dtype=jnp.int32)
    phase_index = positions[:, None] * positions[None, :] % grid_size
    angle_value = phase_index.astype(jnp.float32) * (2.0 * math.pi / grid_size)
    return jnp.concatenate([jnp.cos(angle_value), jnp.sin(angle_value)], axis=0).astype(
        jnp.bfloat16
    )


def shards(
    valence_orbitals,
    conduction_orbitals,
    valence_energy,
    conduction_energy,
    valence_select,
    shifted_index,
    wave_vectors,
    frequency,
):
    grid_size = valence_orbitals.shape[2]
    slab_width = valence_orbitals.shape[3]
    kpoint_count = lax.axis_size("ka")
    band_count = lax.axis_size("band")
    kpoint_rank = lax.axis_index("ka")
    band_rank = lax.axis_index("band")
    vector_count = wave_vectors.shape[1]
    block_rows = vector_count // (kpoint_count * band_count)
    share_size = vector_count // band_count
    permuted = (
        wave_vectors.reshape(3, kpoint_count, band_count, block_rows)
        .transpose(0, 2, 1, 3)
        .reshape(3, vector_count)
    )
    wrapped = jnp.mod(permuted, grid_size)
    twice = 2 * grid_size
    first_index = wrapped[1] * twice + wrapped[2]
    second_index = (grid_size + wrapped[1]) * twice + grid_size + wrapped[2]
    third_index = wrapped[1] * twice + grid_size + wrapped[2]
    fourth_index = (grid_size + wrapped[1]) * twice + wrapped[2]
    plane_coord = band_rank * slab_width + jnp.arange(slab_width, dtype=jnp.int32)
    plane_phase = wrapped[0][None, :] * plane_coord[:, None] % grid_size
    plane_angle = plane_phase.astype(jnp.float32) * (2.0 * math.pi / grid_size)
    norm_scale = float(grid_size) ** (-1.5)
    plane_cos = jnp.cos(plane_angle) * norm_scale
    plane_sin = jnp.sin(plane_angle) * norm_scale
    depth_table = depth_matrix(grid_size)
    column_table = column_matrix(grid_size)
    selected = jnp.take(valence_orbitals[0], valence_select[0], axis=0)
    selected_count = selected.shape[0]
    val_energies = jnp.take(valence_energy[0], valence_select[0])
    partner = shifted_index[kpoint_rank]
    cond_energies = lax.dynamic_index_in_dim(conduction_energy, partner, 0, keepdims=False)
    energy_gap = val_energies[None, :] - cond_energies[:, None]
    weight = (
        2.0
        * energy_gap
        / (energy_gap * energy_gap + frequency[0] * frequency[0])
        / (kpoint_count * selected_count)
    )

    def item_terms(columns):
        cond_real = columns[..., :grid_size].astype(jnp.float32)
        cond_imag = columns[..., grid_size:].astype(jnp.float32)
        val_real = selected[..., :grid_size].astype(jnp.float32)
        val_imag = selected[..., grid_size:].astype(jnp.float32)
        pair_values = jnp.concatenate(
            [
                val_real * cond_real[None] + val_imag * cond_imag[None],
                val_real * cond_imag[None] - val_imag * cond_real[None],
            ],
            axis=-1,
        ).astype(jnp.bfloat16)
        spectrum = jnp.dot(
            pair_values.reshape(-1, twice), depth_table, preferred_element_type=jnp.float32
        )
        spectrum = spectrum.astype(jnp.bfloat16).reshape(pair_values.shape)
        mixed_part = jnp.einsum(
            "ky,nyxc->nxkc", column_table, spectrum, preferred_element_type=jnp.float32
        )
        flat_view = mixed_part.reshape(selected_count, slab_width, twice * twice)
        real_cols = jnp.take(flat_view, first_index, axis=2) + jnp.take(
            flat_view, second_index, axis=2
        )
        imag_cols = jnp.take(flat_view, third_index, axis=2) - jnp.take(
            flat_view, fourth_index, axis=2
        )
        density_real = jnp.sum(plane_cos[None] * real_cols + plane_sin[None] * imag_cols, axis=1)
        density_imag = jnp.sum(plane_cos[None] * imag_cols - plane_sin[None] * real_cols, axis=1)
        return jnp.stack([density_real, density_imag])

    reordered = jnp.take(conduction_orbitals, shifted_index, axis=0)
    partial_value = lax.map(
        item_terms, lax.all_to_all(reordered, "ka", split_axis=0, concat_axis=2, tiled=True)[0]
    )
    summed = lax.psum(partial_value.astype(jnp.bfloat16), "band")
    own_share = lax.dynamic_slice_in_dim(summed, band_rank * share_size, share_size, 3)
    weighted = (weight[:, None, :, None] * own_share.astype(jnp.float32)).astype(jnp.bfloat16)
    contract_dims = (((0, 1, 2), (0, 1, 2)), ((), ()))
    swapped = jnp.stack([weighted[:, 1], -weighted[:, 0]], axis=1)
    real_rows = lax.dot_general(weighted, summed, contract_dims, preferred_element_type=jnp.float32)
    imag_rows = lax.dot_general(swapped, summed, contract_dims, preferred_element_type=jnp.float32)
    chi_block = lax.psum_scatter(
        jnp.stack([real_rows, imag_rows], axis=1).astype(jnp.bfloat16),
        "ka",
        scatter_dimension=0,
        tiled=True,
    ).astype(jnp.float32)
    chi_block = chi_block.reshape(block_rows, 2, band_count, kpoint_count, block_rows).transpose(
        0, 1, 3, 2, 4
    )
    chi_block = chi_block.reshape(block_rows, 2, vector_count)
    return chi_block.transpose(1, 0, 2)


def solution(mesh):
    in_specs = (
        P("ka", None, None, "band", None),
        P(None, None, "ka", "band", None),
        P("ka", None),
        P(),
        P("ka", None),
        P(),
        P(),
        P(),
    )
    out_specs = P(None, ("ka", "band"), None)
    return jax.shard_map(shards, mesh=mesh, in_specs=in_specs, out_specs=out_specs, check_vma=False)
```

profile of v0, /device:TPU:8, one launch (start us, length us, event | category | flops | bytes accessed | tf_op | source)
XLA Modules:
  0.0 472.1 jit_solution(15775231682070053295)
XLA Ops:
  6.5 0.7 compare_select_fusion.4
  7.2 0.7 compare_and_fusion.4
  8.5 0.8 bitcast_select_fusion
  9.3 11.3 %all-to-all-start = ((bf16[32,1,2,8,128]{4,3,2,1,0:T(8,128)(2,1)}), bf16[32,1,2,8,128]{4,3,2,1,0:T(8,128)(2,1)S(1)}, u32[]{:S(2)}, u32[]{:S(2)}) async-start(bf16[32,1,2,8,128]{4,3,2,1,0:T(8,128)(2,1)} %bitcast_select_fusion), calls=%async_computation | async-start | bytes 262144 | tf_op jit(solution)/shard_map/all_to_all | solution.py:111
  20.6 0.7 fusion.38
  21.3 0.7 compare_and_fusion.5
  22.1 1.0 reshape.231
  23.5 4.3 gather_fusion.1
  27.9 1.9 broadcast_select_fusion
  32.5 1.3 copy.35
  33.9 0.7 gather_fusion
  35.8 0.7 constant_dynamic-slice_fusion
  36.6 1.7 fusion.1
  38.3 1.3 convolution_convert_fusion
  39.7 4.6 convolution_bitcast_fusion
  44.2 49.9 %copy.44 = f32[16,8,128,128]{0,1,3,2:T(8,128)} copy(f32[16,8,128,128]{2,3,1,0:T(8,128)} %convolution_bitcast_fusion) | data formatting | bytes 16777216 | tf_op jit(solution)/shard_map/while/body/eval_jaxpr/reshape | solution.py:98
  94.1 33.5 %gather_fusion.6 = f32[2048,16,8]{1,2,0:T(8,128)} fusion(f32[16,8,16384]{0,1,2:T(8,128)} %bitcast.41, s32[2048]{0:T(1024)S(1)} %get-tuple-element.67), kind=kCustom, calls=%fused_computation.3.clone | custom fusion | bytes 2105344 | tf_op jit(solution)/shard_map/while/body/eval_jaxpr/jit(_take)/gather | solution.py:102
  127.6 33.6 %gather_fusion.3 = f32[2048,16,8]{1,2,0:T(8,128)} fusion(f32[16,8,16384]{0,1,2:T(8,128)} %bitcast.41, s32[2048]{0:T(1024)S(1)} %get-tuple-element.57), kind=kCustom, calls=%fused_computation.clone | custom fusion | bytes 2105344 | tf_op jit(solution)/shard_map/while/body/eval_jaxpr/jit(_take)/gather | solution.py:99
  161.3 33.7 %gather_fusion.5 = f32[2048,16,8]{1,2,0:T(8,128)} fusion(f32[16,8,16384]{0,1,2:T(8,128)} %bitcast.41, s32[2048]{0:T(1024)S(1)} %get-tuple-element.56), kind=kCustom, calls=%fused_computation.2.clone | custom fusion | bytes 2105344 | tf_op jit(solution)/shard_map/while/body/eval_jaxpr/jit(_take)/gather | solution.py:102
  195.0 33.5 %gather_fusion.4 = f32[2048,16,8]{1,2,0:T(8,128)} fusion(f32[16,8,16384]{0,1,2:T(8,128)} %bitcast.41, s32[2048]{0:T(1024)S(1)} %get-tuple-element.66), kind=kCustom, calls=%fused_computation.1.clone | custom fusion | bytes 2105344 | tf_op jit(solution)/shard_map/while/body/eval_jaxpr/jit(_take)/gather | solution.py:99
  228.5 21.9 %add_reduce_fusion = (bf16[16,2048]{0,1:T(8,128)(2,1)S(1)}, bf16[16,2048]{0,1:T(8,128)(2,1)S(1)}) fusion(f32[8,2048]{0,1:T(8,128)S(1)} %copy-done.3, f32[8,2048]{0,1:T(8,128)S(1)} %copy.30, f32[2048,16,8]{1,2,0:T(8,128)} %gather_fusion.4, pred[2048]{0:T(1024)(128)(4,1)S(1)} %get-tuple-element.64, f32[2048,16,8]{1,2,0:T(8,128)} %gather_fusion.3, ...), kind=kLoop, calls=%fused_computation.11 | loop fusion | flops 3604480 | bytes 4464640 | tf_op jit(solution)/shard_map/while/body/eval_jaxpr/reduce_sum | solution.py:105
  250.8 0.7 pad_maximum_fusion
  251.7 0.7 multiply_bitcast_fusion
  252.4 77.7 %all-reduce.2.cloned.1.call-done = bf16[1,2,16,2048]{3,2,1,0:T(8,128)(2,1)} async-done(((bf16[1,2,16,2048]{3,2,1,0:T(8,128)(2,1)}), bf16[1,2,16,2048]{3,2,1,0:T(8,128)(2,1)}) %all-reduce.2.cloned.1.call-update) | async-done | bytes 131088 | tf_op jit(solution)/shard_map/psum | solution.py:113
  330.1 0.8 multiply_convert_fusion
  330.9 1.4 fusion.7
  332.3 1.4 fusion.6
  333.8 1.5 copy.46
  335.3 121.5 %reduce-scatter.4.cloned.1.call-done = bf16[8,4096]{1,0:T(8,128)(2,1)} async-done(((bf16[256,4096]{1,0:T(8,128)(2,1)}), bf16[8,4096]{1,0:T(8,128)(2,1)}) %reduce-scatter.4.cloned.1.call-update) | async-done | bytes 65552
  456.8 2.0 reshape.241
  458.9 3.0 copy.40
  461.8 3.4 reshape.240
  (39 shorter events, 3.6 us)
Async XLA Ops:
  6.5 1.4 copy-start
  9.3 27.2 %all-to-all-start = ((bf16[32,1,2,8,128]{4,3,2,1,0:T(8,128)(2,1)}), bf16[32,1,2,8,128]{4,3,2,1,0:T(8,128)(2,1)S(1)}, u32[]{:S(2)}, u32[]{:S(2)}) async-start(bf16[32,1,2,8,128]{4,3,2,1,0:T(8,128)(2,1)} %bitcast_select_fusion), calls=%async_computation | async-start | bytes 262144 | tf_op jit(solution)/shard_map/all_to_all | solution.py:111
  20.6 309.5 %all-reduce.2.cloned.1.call-start = ((), (), s32[]{:S(2)}) async-start(), calls=%async_computation.2 | async-start | bytes 262144 | tf_op jit(solution)/shard_map/psum | solution.py:113
  23.5 6.8 %copy-start.5 = (s32[32]{0:T(128)S(1)}, s32[32]{0:T(128)}, u32[]{:S(2)}) copy-start(s32[32]{0:T(128)} %param.15) | copy-start | bytes 388
  27.9 6.0 %copy-start.2 = (f32[1,32]{1,0:T(1,128)S(1)}, f32[1,32]{1,0:T(1,128)}, u32[]{:S(2)}) copy-start(f32[1,32]{1,0:T(1,128)} %param.12) | copy-start | bytes 388
  27.9 7.9 %copy-start.6 = (f32[32,1]{0,1:T(1,128)S(1)}, f32[32,1]{0,1:T(1,128)}, u32[]{:S(2)}) copy-start(f32[32,1]{0,1:T(1,128)} %param.13) | copy-start | bytes 388
  94.1 134.4 %copy-start.3 = (f32[8,2048]{0,1:T(8,128)S(1)}, f32[8,2048]{0,1:T(8,128)}, u32[]{:S(2)}) copy-start(f32[8,2048]{0,1:T(8,128)} %copy.35) | copy-start | bytes 196612
  228.5 23.2 %copy-start.4 = (s32[1,16]{1,0:T(1,128)S(1)}, s32[1,16]{1,0:T(1,128)}, u32[]{:S(2)}) copy-start(s32[1,16]{1,0:T(1,128)} %param.14) | copy-start | bytes 196
  251.5 205.4 %reduce-scatter.4.cloned.1.call-start = ((), (), s32[]{:S(2)}) async-start(), calls=%async_computation.3 | async-start | bytes 2162688
  456.8 8.4 %copy-start.1 = (bf16[32,1,2,8,128]{4,3,2,1,0:T(8,128)(2,1)S(1)}, bf16[32,1,2,8,128]{4,3,2,1,0:T(8,128)(2,1)}, u32[]{:S(2)}) copy-start(bf16[32,1,2,8,128]{4,3,2,1,0:T(8,128)(2,1)} %param.11) | copy-start | bytes 393220
Sparse Core Ops, SparseCore 0:
  251.6 78.4 all-reduce.1
  335.4 121.3 reduce-scatter.3
where the time goes:
time: 475 us; the launch traced here: 472 us
  local copies, waits for them, and re-layouts  204 us (43%)
  waiting for transfers between devices  199 us (42%)
  other arithmetic  32.1 us (7%)
  between operations  16.2 us (3%)
  starting transfers between devices  11.6 us (2%)
  matrix products  8.6 us (2%)
    unnamed x3, waiting for transfers between devices  122 us
    psum x1, waiting for transfers between devices, shards(): summed = lax.psum(partial_value.astype(jnp.bfloat16), 'band')  77.7 us
    reshape x1, local copies, waits for them, and re-layouts, item_terms(): flat_view = mixed_part.reshape(selected_count, slab_width, twice * twice)  49.9 us
    gather x1, local copies, waits for them, and re-layouts, item_terms(): jnp.take(flat_view, third_index, axis=2)  33.7 us
    gather x1, local copies, waits for them, and re-layouts, item_terms(): jnp.take(flat_view, first_index, axis=2)  33.6 us
    gather x1, local copies, waits for them, and re-layouts, item_terms(): jnp.take(flat_view, second_index, axis=2)  33.5 us
    gather x1, local copies, waits for them, and re-layouts, item_terms(): jnp.take(flat_view, fourth_index, axis=2)  33.5 us
    reduce_sum x1, other arithmetic, item_terms(): jnp.sum(plane_cos[None] * real_cols + plane_sin[None] * imag_cols, axis=1)  21.9 us
  transfers between devices with their start and end apart: 3, of which 2 were waited for; matrix products, arithmetic and copies ran while one was open for 3% of the time, Pallas kernels for 0%

commit v1 on v0

--- a/solution.py
+++ b/solution.py
@@ -110,7 +110,7 @@
     partial_value = lax.map(
         item_terms, lax.all_to_all(reordered, "ka", split_axis=0, concat_axis=2, tiled=True)[0]
     )
-    summed = lax.psum(partial_value.astype(jnp.bfloat16), "band")
+    summed = jnp.sum(lax.all_gather(partial_value.astype(jnp.bfloat16), "band"), axis=0)
     own_share = lax.dynamic_slice_in_dim(summed, band_rank * share_size, share_size, 3)
     weighted = (weight[:, None, :, None] * own_share.astype(jnp.float32)).astype(jnp.bfloat16)
     contract_dims = (((0, 1, 2), (0, 1, 2)), ((), ()))

time: 475 us -> 432 us (0.909)
  waiting for transfers between devices: 199 us -> 157 us
    psum x1 -> x0, waiting for transfers between devices: 77.7 us -> none  [shards(): summed = lax.psum(partial_value.astype(jnp.bfloat16), 'band')]
    all_gather x0 -> x1, waiting for transfers between devices: none -> 34.9 us  [shards(): lax.all_gather(partial_value.astype(jnp.bfloat16), 'band')]
  transfers between devices with their start and end apart: 3 -> 3, of which waited for: 2 -> 3; matrix products, arithmetic and copies ran while one was open for 3% -> 3% of each run, Pallas kernels for 0% -> 0%
where the time goes in v1:
time: 432 us; the launch traced here: 428 us
  local copies, waits for them, and re-layouts  204 us (47%)
  waiting for transfers between devices  157 us (36%)
  other arithmetic  32.6 us (8%)
  between operations  16 us (4%)
  starting transfers between devices  11.6 us (3%)
  matrix products  6.85 us (2%)
    unnamed x3, waiting for transfers between devices  121 us
    reshape x1, local copies, waits for them, and re-layouts, item_terms(): flat_view = mixed_part.reshape(selected_count, slab_width, twice * twice)  49.9 us
    all_gather x1, waiting for transfers between devices, shards(): lax.all_gather(partial_value.astype(jnp.bfloat16), 'band')  34.9 us
    gather x1, local copies, waits for them, and re-layouts, item_terms(): jnp.take(flat_view, third_index, axis=2)  33.7 us
    gather x1, local copies, waits for them, and re-layouts, item_terms(): jnp.take(flat_view, first_index, axis=2)  33.6 us
    gather x1, local copies, waits for them, and re-layouts, item_terms(): jnp.take(flat_view, second_index, axis=2)  33.5 us
    gather x1, local copies, waits for them, and re-layouts, item_terms(): jnp.take(flat_view, fourth_index, axis=2)  33.5 us
    reduce_sum x1, other arithmetic, item_terms(): jnp.sum(plane_cos[None] * real_cols + plane_sin[None] * imag_cols, axis=1)  21.9 us
  transfers between devices with their start and end apart: 3, of which 3 were waited for; matrix products, arithmetic and copies ran while one was open for 3% of the time, Pallas kernels for 0%

profile of v1, /device:TPU:8, one launch (start us, length us, event | category | flops | bytes accessed | tf_op | source)
XLA Modules:
  0.0 428.3 jit_solution(132215848327088559)
XLA Ops:
  6.5 0.7 compare_select_fusion.4
  7.2 0.7 compare_and_fusion.4
  7.9 0.6 gather_fusion.2
  8.5 0.8 bitcast_select_fusion
  9.3 11.3 %all-to-all-start = ((bf16[32,1,2,8,128]{4,3,2,1,0:T(8,128)(2,1)}), bf16[32,1,2,8,128]{4,3,2,1,0:T(8,128)(2,1)S(1)}, u32[]{:S(2)}, u32[]{:S(2)}) async-start(bf16[32,1,2,8,128]{4,3,2,1,0:T(8,128)(2,1)} %bitcast_select_fusion), calls=%async_computation | async-start | bytes 262144 | tf_op jit(solution)/shard_map/all_to_all | solution.py:111
  20.6 0.7 fusion.36
  21.3 0.7 compare_and_fusion.5
  22.1 1.0 reshape.239
  23.5 4.3 %gather_fusion.1 = bf16[16,64,8,128]{3,2,1,0:T(8,128)(2,1)} fusion(bf16[32,64,8,128]{3,2,1,0:T(8,128)(2,1)} %bitcast.116, s32[1024]{0:T(1024)S(1)} %pad_clamp_fusion.1), kind=kCustom, calls=%fused_computation.5 | custom fusion | bytes 4194368 | tf_op jit(solution)/shard_map/jit(_take)/gather | solution.py:66
  27.9 1.8 broadcast_select_fusion
  30.6 1.3 copy.44
  31.9 0.6 all-to-all-done
  32.6 1.7 fusion.1
  34.4 1.3 convolution_convert_fusion
  35.7 4.6 %convolution_bitcast_fusion = f32[16,8,128,128]{2,3,1,0:T(8,128)} fusion(bf16[16,64,8,128]{3,2,1,0:T(8,128)(2,1)S(1)} %bitcast.109, bf16[64,64]{0,1:T(8,128)(2,1)S(1)} %fusion.34, bf16[64,64]{0,1:T(8,128)(2,1)S(1)} %get-tuple-element.69), kind=kOutput, calls=%fused_computation.20 | convolution fusion | flops 268468224 | bytes 10502144 | tf_op jit(solution)/shard_map/while/body/eval_jaxpr/ky,nyxc->nxkc/dot_general | solution.py:95
  40.3 49.9 %copy.53 = f32[16,8,128,128]{0,1,3,2:T(8,128)} copy(f32[16,8,128,128]{2,3,1,0:T(8,128)} %convolution_bitcast_fusion) | data formatting | bytes 16777216 | tf_op jit(solution)/shard_map/while/body/eval_jaxpr/reshape | solution.py:98
  90.1 33.5 %gather_fusion.6 = f32[2048,16,8]{1,2,0:T(8,128)} fusion(f32[16,8,16384]{0,1,2:T(8,128)} %bitcast.40, s32[2048]{0:T(1024)S(1)} %get-tuple-element.67), kind=kCustom, calls=%fused_computation.3.clone | custom fusion | bytes 2105344 | tf_op jit(solution)/shard_map/while/body/eval_jaxpr/jit(_take)/gather | solution.py:102
  123.7 33.6 %gather_fusion.3 = f32[2048,16,8]{1,2,0:T(8,128)} fusion(f32[16,8,16384]{0,1,2:T(8,128)} %bitcast.40, s32[2048]{0:T(1024)S(1)} %get-tuple-element.57), kind=kCustom, calls=%fused_computation.clone | custom fusion | bytes 2105344 | tf_op jit(solution)/shard_map/while/body/eval_jaxpr/jit(_take)/gather | solution.py:99
  157.3 33.7 %gather_fusion.5 = f32[2048,16,8]{1,2,0:T(8,128)} fusion(f32[16,8,16384]{0,1,2:T(8,128)} %bitcast.40, s32[2048]{0:T(1024)S(1)} %get-tuple-element.56), kind=kCustom, calls=%fused_computation.2.clone | custom fusion | bytes 2105344 | tf_op jit(solution)/shard_map/while/body/eval_jaxpr/jit(_take)/gather | solution.py:102
  191.0 33.5 %gather_fusion.4 = f32[2048,16,8]{1,2,0:T(8,128)} fusion(f32[16,8,16384]{0,1,2:T(8,128)} %bitcast.40, s32[2048]{0:T(1024)S(1)} %get-tuple-element.66), kind=kCustom, calls=%fused_computation.1.clone | custom fusion | bytes 2105344 | tf_op jit(solution)/shard_map/while/body/eval_jaxpr/jit(_take)/gather | solution.py:99
  224.6 21.9 %add_reduce_fusion = (bf16[16,2048]{0,1:T(8,128)(2,1)S(1)}, bf16[16,2048]{0,1:T(8,128)(2,1)S(1)}) fusion(f32[8,2048]{0,1:T(8,128)S(1)} %copy-done.3, f32[8,2048]{0,1:T(8,128)S(1)} %copy.39, f32[2048,16,8]{1,2,0:T(8,128)} %gather_fusion.4, pred[2048]{0:T(1024)(128)(4,1)S(1)} %get-tuple-element.64, f32[2048,16,8]{1,2,0:T(8,128)} %gather_fusion.3, ...), kind=kLoop, calls=%fused_computation.11 | loop fusion | flops 3604480 | bytes 4464640 | tf_op jit(solution)/shard_map/while/body/eval_jaxpr/reduce_sum | solution.py:105
  246.8 0.7 pad_maximum_fusion
  247.7 0.6 dynamic_slice.11
  249.5 0.7 gather_fusion
  252.0 0.6 multiply_bitcast_fusion
  252.5 34.9 %all-gather.2.cloned.1.call-done = bf16[8,1,2,16,2048]{4,3,2,1,0:T(8,128)(2,1)} async-done(((bf16[1,1,2,16,2048]{4,3,2,1,0:T(8,128)(2,1)}), bf16[8,1,2,16,2048]{4,3,2,1,0:T(8,128)(2,1)}) %all-gather.2.cloned.1.call-update) | async-done | bytes 1048592 | tf_op jit(solution)/shard_map/all_gather | solution.py:113
  287.5 1.4 reduce_sum.34
  290.1 1.5 copy.55
  291.6 121.4 %reduce-scatter.4.cloned.1.call-done = bf16[8,4096]{1,0:T(8,128)(2,1)} async-done(((bf16[256,4096]{1,0:T(8,128)(2,1)}), bf16[8,4096]{1,0:T(8,128)(2,1)}) %reduce-scatter.4.cloned.1.call-update) | async-done | bytes 65552
  413.0 2.0 reshape.247
  415.0 3.0 copy.49
  418.0 3.4 reshape.246
  (40 shorter events, 4.0 us)
Async XLA Ops:
  6.5 1.4 copy-start
  9.3 23.3 %all-to-all-start = ((bf16[32,1,2,8,128]{4,3,2,1,0:T(8,128)(2,1)}), bf16[32,1,2,8,128]{4,3,2,1,0:T(8,128)(2,1)S(1)}, u32[]{:S(2)}, u32[]{:S(2)}) async-start(bf16[32,1,2,8,128]{4,3,2,1,0:T(8,128)(2,1)} %bitcast_select_fusion), calls=%async_computation | async-start | bytes 262144 | tf_op jit(solution)/shard_map/all_to_all | solution.py:111
  20.6 266.9 %all-gather.2.cloned.1.call-start = ((), (), s32[]{:S(2)}) async-start(), calls=%async_computation.2 | async-start | bytes 1179648 | tf_op jit(solution)/shard_map/all_gather | solution.py:113
  90.1 134.4 %copy-start.3 = (f32[8,2048]{0,1:T(8,128)S(1)}, f32[8,2048]{0,1:T(8,128)}, u32[]{:S(2)}) copy-start(f32[8,2048]{0,1:T(8,128)} %copy.44) | copy-start | bytes 196612
  224.5 23.2 %copy-start.5 = (s32[32]{0:T(128)S(1)}, s32[32]{0:T(128)}, u32[]{:S(2)}) copy-start(s32[32]{0:T(128)} %param.15) | copy-start | bytes 388
  224.5 24.9 %copy-start.2 = (f32[1,32]{1,0:T(1,128)S(1)}, f32[1,32]{1,0:T(1,128)}, u32[]{:S(2)}) copy-start(f32[1,32]{1,0:T(1,128)} %param.12) | copy-start | bytes 388
  224.5 26.8 %copy-start.6 = (f32[32,1]{0,1:T(1,128)S(1)}, f32[32,1]{0,1:T(1,128)}, u32[]{:S(2)}) copy-start(f32[32,1]{0,1:T(1,128)} %param.13) | copy-start | bytes 388
  224.6 27.4 %copy-start.4 = (s32[1,16]{1,0:T(1,128)S(1)}, s32[1,16]{1,0:T(1,128)}, u32[]{:S(2)}) copy-start(s32[1,16]{1,0:T(1,128)} %param.14) | copy-start | bytes 196
  247.5 165.5 %reduce-scatter.4.cloned.1.call-start = ((), (), s32[]{:S(2)}) async-start(), calls=%async_computation.3 | async-start | bytes 2162688
  413.0 8.4 %copy-start.1 = (bf16[32,1,2,8,128]{4,3,2,1,0:T(8,128)(2,1)S(1)}, bf16[32,1,2,8,128]{4,3,2,1,0:T(8,128)(2,1)}, u32[]{:S(2)}) copy-start(bf16[32,1,2,8,128]{4,3,2,1,0:T(8,128)(2,1)} %param.11) | copy-start | bytes 393220
Sparse Core Ops, SparseCore 0:
  247.6 39.8 all-gather.1
  291.7 121.2 reduce-scatter.3
